TPU v7x, 32 devices: a whole 2x2x4 slice. The times are simulated.
32 devices in a mesh: layer: 4 (over y, core), front: 8 (over z, x).
Axes of the slice: x: 2, y: 2, z: 4, core: 2. Of those that a mesh axis runs over, the one named last changes fastest.
Arguments:
- sources_down: float32 [4, 8, 2, 32, 256], P('layer', 'front'), may hold values from -6 to 6
- sources_up: float32 [4, 8, 2, 32, 256], P('layer', 'front'), may hold values from -6 to 6
- leaf_inverse: float32 [4, 8, 2, 256, 256], P('layer', 'front'), may hold values from -0.25 to 0.25
- coupling: float32 [4, 8, 2, 512, 256], P('layer', 'front'), may hold values from -0.25 to 0.25
- sep_inverse: float32 [4, 8, 2, 256, 256], P('layer', 'front'), may hold values from -0.25 to 0.25
- inject_top: float32 [4, 8, 2, 128, 256], P('layer', 'front'), may hold values from -0.125 to 0.125
- inject_bottom: float32 [4, 8, 2, 128, 256], P('layer', 'front'), may hold values from -0.125 to 0.125
- targets: int32 [4, 8, 16, 1], P('layer', 'front'), may hold values from 0 to 7; in each aligned block of 16 rows (0 to 15, 16 to 31, ..., all dimensions but the last counted through in order) at most 2 rows name the same one
- offsets: int32 [4, 8, 16], P('layer', 'front'), may hold values from 0 to 7
Outputs:
- field_down: float32 [4, 8, 2, 32, 256], P('layer', 'front')
- field_up: float32 [4, 8, 2, 32, 256], P('layer', 'front')
Inputs may be any that keep to these rules, and one draw needn't show every extreme that they name: `targets`: the 16 blocks of one leaf name one separator at most 2 times, and in every draw some leaf names one separator exactly 2 times.
All inputs are finite; a program needn't handle non-finite values.
Results may differ from a plain program's by a relative error of at most 0.00019.
Values sent between devices are 32-bit elements; how exact they have to be, the bound alone decides.
A program may use at most 64 MiB of HBM per device.

v0:
```python
import jax
import jax.numpy as jnp
from jax import lax
from jax.sharding import PartitionSpec as P

P_SIZE = 256
Q = 256
TR = 128
RB = 32
S = 32
NB = 16
QB = 8


precise = lax.Precision.HIGHEST


def passed_along(value, axis, steps):
    count = lax.axis_size(axis)
    initial, last = (max(0, -steps), min(count, count - steps))
    return lax.ppermute(value, axis, [(source, source + steps) for source in range(initial, last)])


def complex_product(pattern, first, second):
    real_part = jnp.einsum(pattern, first[0], second[0], precision=precise) - jnp.einsum(
        pattern, first[1], second[1], precision=precise
    )
    imag_part = jnp.einsum(pattern, first[0], second[1], precision=precise) + jnp.einsum(
        pattern, first[1], second[0], precision=precise
    )
    return (real_part, imag_part)


def block_ranks(target_list):
    count = target_list.shape[0]
    same = target_list[:, None] == target_list[None, :]
    earlier = jnp.arange(count)[None, :] < jnp.arange(count)[:, None]
    return jnp.sum(same & earlier, axis=1)


def to_rows(blocked, columns):
    return blocked.transpose(1, 0, 2).reshape(columns, Q)


def to_blocks(rows, columns):
    return rows.reshape(columns, QB, RB).transpose(1, 0, 2)


def front_solve(rhs, leaf_matrix, coupling_rows, sep_matrix, target_list, offset_list):
    leaves = lax.axis_size("front")
    capacity = max(2, (NB + leaves - 1) // leaves)
    columns = rhs.shape[1]
    breadth = columns * 2 * RB
    interior = complex_product("cq,pq->cp", rhs, leaf_matrix)
    coupling_blocks = coupling_rows.reshape(2, NB, RB, P_SIZE)
    update = complex_product("cp,nrp->ncr", interior, coupling_blocks)
    packed = jnp.concatenate(update, axis=2).reshape(NB, breadth)
    ranks = block_ranks(target_list)
    slot_owner = jnp.arange(leaves * capacity) // capacity
    slot_rank = jnp.arange(leaves * capacity) % capacity
    select = (target_list[None, :] == slot_owner[:, None]) & (ranks[None, :] == slot_rank[:, None])
    select_float = select.astype(jnp.float32)
    outgoing = jnp.dot(select_float, packed, precision=precise).reshape(
        leaves, capacity, columns, 2 * RB
    )
    filled = jnp.sum(select.astype(jnp.int32), axis=1)
    slot_offset = jnp.sum(jnp.where(select, offset_list[None, :], 0), axis=1) + QB * (1 - filled)
    slot_offset = slot_offset.reshape(leaves, capacity)
    arrived, arrived_offset = (
        lax.all_to_all(outgoing, "front", split_axis=0, concat_axis=0, tiled=True),
        lax.all_to_all(slot_offset, "front", split_axis=0, concat_axis=0, tiled=True),
    )
    placing = (arrived_offset.reshape(-1)[None, :] == jnp.arange(QB)[:, None]).astype(jnp.float32)
    assembled = jnp.dot(
        placing, arrived.reshape(leaves * capacity, breadth), precision=precise
    ).reshape(QB, columns, 2 * RB)
    sep_rhs = (to_rows(assembled[:, :, :RB], columns), to_rows(assembled[:, :, RB:], columns))
    solved = complex_product("cs,qs->cq", sep_rhs, sep_matrix)
    solved_packed = jnp.concatenate(
        [to_blocks(solved[0], columns), to_blocks(solved[1], columns)], axis=2
    ).reshape(QB, breadth)
    reply = jnp.einsum("qk,qx->kx", placing, solved_packed, precision=precise).reshape(
        leaves, capacity, columns, 2 * RB
    )
    returned = lax.all_to_all(reply, "front", split_axis=0, concat_axis=0, tiled=True)
    mine = jnp.einsum(
        "kn,kx->nx", select_float, returned.reshape(leaves * capacity, breadth), precision=precise
    ).reshape(NB, columns, 2 * RB)
    pushed = complex_product("ncr,nrp->cp", (mine[:, :, :RB], mine[:, :, RB:]), coupling_blocks)
    correction = complex_product("cq,pq->cp", pushed, leaf_matrix)
    return jnp.stack([interior[0] + correction[0], interior[1] + correction[1]])


def feed(sources, mapping, trace, piece_index, pieces, piece_width):
    start = jnp.clip(piece_index, 0, pieces - 1) * piece_width
    local = lax.dynamic_slice_in_dim(sources, start, piece_width, 1)
    injected = complex_product("ct,tp->cp", trace, mapping)
    return jnp.stack([local[0] + injected[0], local[1] + injected[1]])


def store(output, part, piece_index, pieces, piece_width):
    valid = (piece_index >= 0) & (piece_index < pieces)
    start = jnp.clip(piece_index, 0, pieces - 1) * piece_width
    current = lax.dynamic_slice_in_dim(output, start, piece_width, 1)
    return lax.dynamic_update_slice_in_dim(output, jnp.where(valid, part, current), start, 1)


def send_down(part):
    return passed_along(part[:, :, P_SIZE - TR :], "layer", 1)


def send_up(part):
    return passed_along(part[:, :, :TR], "layer", -1)


def body(
    sources_down,
    sources_up,
    leaf_inverse,
    coupling,
    sep_inverse,
    inject_top,
    inject_bottom,
    targets,
    offsets,
):
    depth = lax.axis_size("layer")
    depth_index = lax.axis_index("layer")
    leaf_matrix = leaf_inverse[0, 0]
    coupling_rows = coupling[0, 0]
    sep_matrix = sep_inverse[0, 0]
    top_map = inject_top[0, 0]
    bottom_map = inject_bottom[0, 0]
    down_sources = sources_down[0, 0]
    up_sources = sources_up[0, 0]
    target_list = targets[0, 0, :, 0]
    offset_list = offsets[0, 0]
    pieces = 2
    piece_width = S // pieces
    sections = pieces + depth - 1
    blank_trace = jnp.zeros((2, piece_width, TR), jnp.float32)
    blank_field = jnp.zeros((2, S, P_SIZE), jnp.float32)

    def solve_piece(rhs):
        return front_solve(rhs, leaf_matrix, coupling_rows, sep_matrix, target_list, offset_list)

    def joint_section(section, carry):
        out_down, out_up, trace_down, trace_up = carry
        piece_down = section - depth_index
        piece_up = section - (depth - 1 - depth_index)
        rhs = jnp.concatenate(
            [
                feed(down_sources, top_map, trace_down, piece_down, pieces, piece_width),
                feed(up_sources, bottom_map, trace_up, piece_up, pieces, piece_width),
            ],
            axis=1,
        )
        field = solve_piece(rhs)
        down_part = field[:, :piece_width]
        up_part = field[:, piece_width:]
        out_down = store(out_down, down_part, piece_down, pieces, piece_width)
        out_up = store(out_up, up_part, piece_up, pieces, piece_width)
        return (out_down, out_up, send_down(down_part), send_up(up_part))

    field_down, field_up, unused_down, unused_up = lax.fori_loop(
        0, sections, joint_section, (blank_field, blank_field, blank_trace, blank_trace)
    )
    return (field_down[None, None], field_up[None, None])


def solution(mesh):
    return jax.shard_map(
        body,
        mesh=mesh,
        in_specs=(
            P("layer", "front", None, None, None),
            P("layer", "front", None, None, None),
            P("layer", "front", None, None, None),
            P("layer", "front", None, None, None),
            P("layer", "front", None, None, None),
            P("layer", "front", None, None, None),
            P("layer", "front", None, None, None),
            P("layer", "front", None, None),
            P("layer", "front", None),
        ),
        out_specs=(P("layer", "front", None, None, None), P("layer", "front", None, None, None)),
        check_vma=False,
    )
```

profile of v0, /device:TPU:0, one launch (start us, length us, event | category | flops | bytes accessed | tf_op | source)
XLA Modules:
  0.0 300.0 jit_solution(10475029171114160733)
XLA Ops:
  1.5 297.9 %while.21 = (s32[]{:T(128)}, f32[2,32,256]{2,1,0:T(8,128)S(1)}, f32[2,32,256]{2,1,0:T(8,128)S(1)}, f32[2,16,128]{2,1,0:T(8,128)S(1)}, f32[2,16,128]{2,1,0:T(8,12...) while((s32[]{:T(128)}, f32[2,32,256]{2,1,0:T(8,128)S(1)}, ...), condition=%wide.region_4.5_spmd, body=%wide.region_0.4_spmd.sunk | while | flops 774141184 | bytes 30714864 | solution.py:165
  2.4 7.3 %all-to-all-start.1 = ((s32[8,1,2]{2,1,0:T(1,128)}), s32[8,1,2]{2,1,0:T(1,128)S(1)}, u32[]{:S(2)}, u32[]{:S(2)}) async-start(s32[8,1,2]{2,1,0:T(1,128)} %bitcast.377), calls=%async_computation.1 | async-start | bytes 8192 | tf_op jit(solution)/shard_map/while/body/eval_jaxpr/all_to_all | solution.py:71
  10.8 1.1 fusion.303
  14.6 1.3 fusion.310
  15.9 1.3 fusion.307
  17.2 1.3 fusion.311
  18.5 1.3 fusion.309
  21.5 6.0 %all-to-all-start = ((f32[8,1,4096]{2,1,0:T(1,128)}), f32[8,1,4096]{2,1,0:T(1,128)S(1)}, u32[]{:S(2)}, u32[]{:S(2)}) async-start(f32[8,1,4096]{2,1,0:T(1,128)} %reshape.305), calls=%async_computation | async-start | bytes 262144 | tf_op jit(solution)/shard_map/while/body/eval_jaxpr/all_to_all | solution.py:70
  28.9 6.0 %all-to-all-done = f32[8,1,4096]{2,1,0:T(1,128)S(1)} async-done(((f32[8,1,4096]{2,1,0:T(1,128)}), f32[8,1,4096]{2,1,0:T(1,128)S(1)}, u32[]{:S(2)}, u32[]{:S(2)}) %all-to-all-start) | async-done | bytes 131104 | tf_op jit(solution)/shard_map/while/body/eval_jaxpr/all_to_all | solution.py:70
  40.9 3.4 %all-to-all-start.2 = ((f32[8,1,4096]{2,1,0:T(1,128)}), f32[8,1,4096]{2,1,0:T(1,128)S(1)}, u32[]{:S(2)}, u32[]{:S(2)}) async-start(f32[8,1,4096]{2,1,0:T(1,128)} %reshape.313), calls=%async_computation.2 | async-start | bytes 262144 | tf_op jit(solution)/shard_map/while/body/eval_jaxpr/all_to_all | solution.py:85
  44.3 7.3 %all-to-all-done.2 = f32[8,1,4096]{2,1,0:T(1,128)S(1)} async-done(((f32[8,1,4096]{2,1,0:T(1,128)}), f32[8,1,4096]{2,1,0:T(1,128)S(1)}, u32[]{:S(2)}, u32[]{:S(2)}) %all-to-all-start.2) | async-done | bytes 131104 | tf_op jit(solution)/shard_map/while/body/eval_jaxpr/all_to_all | solution.py:85
  57.5 1.3 collective-permute-start
  58.8 1.3 collective-permute-start.1
  60.1 3.5 %collective-permute-done.1 = f32[2,16,128]{2,1,0:T(8,128)S(1)} collective-permute-done((f32[2,16,128]{2,1,0:T(8,128)S(1)}, f32[2,16,128]{2,1,0:T(8,128)S(1)}, u32[]{:S(2)}, u32[]{:S(2)}) %collective-permute-start.1) | collective-permute-done | bytes 16416 | tf_op jit(solution)/shard_map/while/body/eval_jaxpr/ppermute | solution.py:21
  64.5 3.3 %all-to-all-start.1 = ((s32[8,1,2]{2,1,0:T(1,128)}), s32[8,1,2]{2,1,0:T(1,128)S(1)}, u32[]{:S(2)}, u32[]{:S(2)}) async-start(s32[8,1,2]{2,1,0:T(1,128)} %bitcast.377), calls=%async_computation.1 | async-start | bytes 8192 | tf_op jit(solution)/shard_map/while/body/eval_jaxpr/all_to_all | solution.py:71
  72.8 1.3 fusion.310
  74.1 1.3 fusion.307
  75.4 1.3 fusion.311
  76.7 1.3 fusion.309
  79.7 5.9 %all-to-all-start = ((f32[8,1,4096]{2,1,0:T(1,128)}), f32[8,1,4096]{2,1,0:T(1,128)S(1)}, u32[]{:S(2)}, u32[]{:S(2)}) async-start(f32[8,1,4096]{2,1,0:T(1,128)} %reshape.305), calls=%async_computation | async-start | bytes 262144 | tf_op jit(solution)/shard_map/while/body/eval_jaxpr/all_to_all | solution.py:70
  86.9 6.0 %all-to-all-done = f32[8,1,4096]{2,1,0:T(1,128)S(1)} async-done(((f32[8,1,4096]{2,1,0:T(1,128)}), f32[8,1,4096]{2,1,0:T(1,128)S(1)}, u32[]{:S(2)}, u32[]{:S(2)}) %all-to-all-start) | async-done | bytes 131104 | tf_op jit(solution)/shard_map/while/body/eval_jaxpr/all_to_all | solution.py:70
  99.0 3.4 %all-to-all-start.2 = ((f32[8,1,4096]{2,1,0:T(1,128)}), f32[8,1,4096]{2,1,0:T(1,128)S(1)}, u32[]{:S(2)}, u32[]{:S(2)}) async-start(f32[8,1,4096]{2,1,0:T(1,128)} %reshape.313), calls=%async_computation.2 | async-start | bytes 262144 | tf_op jit(solution)/shard_map/while/body/eval_jaxpr/all_to_all | solution.py:85
  102.4 8.2 %all-to-all-done.2 = f32[8,1,4096]{2,1,0:T(1,128)S(1)} async-done(((f32[8,1,4096]{2,1,0:T(1,128)}), f32[8,1,4096]{2,1,0:T(1,128)S(1)}, u32[]{:S(2)}, u32[]{:S(2)}) %all-to-all-start.2) | async-done | bytes 131104 | tf_op jit(solution)/shard_map/while/body/eval_jaxpr/all_to_all | solution.py:85
  116.5 1.3 collective-permute-start
  117.9 1.3 collective-permute-start.1
  119.2 3.4 %collective-permute-done.1 = f32[2,16,128]{2,1,0:T(8,128)S(1)} collective-permute-done((f32[2,16,128]{2,1,0:T(8,128)S(1)}, f32[2,16,128]{2,1,0:T(8,128)S(1)}, u32[]{:S(2)}, u32[]{:S(2)}) %collective-permute-start.1) | collective-permute-done | bytes 16416 | tf_op jit(solution)/shard_map/while/body/eval_jaxpr/ppermute | solution.py:21
  123.4 3.3 %all-to-all-start.1 = ((s32[8,1,2]{2,1,0:T(1,128)}), s32[8,1,2]{2,1,0:T(1,128)S(1)}, u32[]{:S(2)}, u32[]{:S(2)}) async-start(s32[8,1,2]{2,1,0:T(1,128)} %bitcast.377), calls=%async_computation.1 | async-start | bytes 8192 | tf_op jit(solution)/shard_map/while/body/eval_jaxpr/all_to_all | solution.py:71
  127.9 1.1 fusion.303
  131.7 1.3 fusion.310
  133.0 1.3 fusion.307
  134.3 1.3 fusion.311
  135.6 1.3 fusion.309
  138.6 5.9 %all-to-all-start = ((f32[8,1,4096]{2,1,0:T(1,128)}), f32[8,1,4096]{2,1,0:T(1,128)S(1)}, u32[]{:S(2)}, u32[]{:S(2)}) async-start(f32[8,1,4096]{2,1,0:T(1,128)} %reshape.305), calls=%async_computation | async-start | bytes 262144 | tf_op jit(solution)/shard_map/while/body/eval_jaxpr/all_to_all | solution.py:70
  145.9 6.0 %all-to-all-done = f32[8,1,4096]{2,1,0:T(1,128)S(1)} async-done(((f32[8,1,4096]{2,1,0:T(1,128)}), f32[8,1,4096]{2,1,0:T(1,128)S(1)}, u32[]{:S(2)}, u32[]{:S(2)}) %all-to-all-start) | async-done | bytes 131104 | tf_op jit(solution)/shard_map/while/body/eval_jaxpr/all_to_all | solution.py:70
  158.0 3.4 %all-to-all-start.2 = ((f32[8,1,4096]{2,1,0:T(1,128)}), f32[8,1,4096]{2,1,0:T(1,128)S(1)}, u32[]{:S(2)}, u32[]{:S(2)}) async-start(f32[8,1,4096]{2,1,0:T(1,128)} %reshape.313), calls=%async_computation.2 | async-start | bytes 262144 | tf_op jit(solution)/shard_map/while/body/eval_jaxpr/all_to_all | solution.py:85
  161.4 8.2 %all-to-all-done.2 = f32[8,1,4096]{2,1,0:T(1,128)S(1)} async-done(((f32[8,1,4096]{2,1,0:T(1,128)}), f32[8,1,4096]{2,1,0:T(1,128)S(1)}, u32[]{:S(2)}, u32[]{:S(2)}) %all-to-all-start.2) | async-done | bytes 131104 | tf_op jit(solution)/shard_map/while/body/eval_jaxpr/all_to_all | solution.py:85
  175.5 1.3 collective-permute-start
  176.8 1.3 collective-permute-start.1
  178.1 3.4 %collective-permute-done.1 = f32[2,16,128]{2,1,0:T(8,128)S(1)} collective-permute-done((f32[2,16,128]{2,1,0:T(8,128)S(1)}, f32[2,16,128]{2,1,0:T(8,128)S(1)}, u32[]{:S(2)}, u32[]{:S(2)}) %collective-permute-start.1) | collective-permute-done | bytes 16416 | tf_op jit(solution)/shard_map/while/body/eval_jaxpr/ppermute | solution.py:21
  182.4 3.3 %all-to-all-start.1 = ((s32[8,1,2]{2,1,0:T(1,128)}), s32[8,1,2]{2,1,0:T(1,128)S(1)}, u32[]{:S(2)}, u32[]{:S(2)}) async-start(s32[8,1,2]{2,1,0:T(1,128)} %bitcast.377), calls=%async_computation.1 | async-start | bytes 8192 | tf_op jit(solution)/shard_map/while/body/eval_jaxpr/all_to_all | solution.py:71
  186.8 1.1 fusion.303
  190.7 1.3 fusion.310
  192.0 1.3 fusion.307
  193.3 1.3 fusion.311
  194.6 1.3 fusion.309
  197.6 5.9 %all-to-all-start = ((f32[8,1,4096]{2,1,0:T(1,128)}), f32[8,1,4096]{2,1,0:T(1,128)S(1)}, u32[]{:S(2)}, u32[]{:S(2)}) async-start(f32[8,1,4096]{2,1,0:T(1,128)} %reshape.305), calls=%async_computation | async-start | bytes 262144 | tf_op jit(solution)/shard_map/while/body/eval_jaxpr/all_to_all | solution.py:70
  204.8 6.0 %all-to-all-done = f32[8,1,4096]{2,1,0:T(1,128)S(1)} async-done(((f32[8,1,4096]{2,1,0:T(1,128)}), f32[8,1,4096]{2,1,0:T(1,128)S(1)}, u32[]{:S(2)}, u32[]{:S(2)}) %all-to-all-start) | async-done | bytes 131104 | tf_op jit(solution)/shard_map/while/body/eval_jaxpr/all_to_all | solution.py:70
  216.9 3.4 %all-to-all-start.2 = ((f32[8,1,4096]{2,1,0:T(1,128)}), f32[8,1,4096]{2,1,0:T(1,128)S(1)}, u32[]{:S(2)}, u32[]{:S(2)}) async-start(f32[8,1,4096]{2,1,0:T(1,128)} %reshape.313), calls=%async_computation.2 | async-start | bytes 262144 | tf_op jit(solution)/shard_map/while/body/eval_jaxpr/all_to_all | solution.py:85
  220.3 8.2 %all-to-all-done.2 = f32[8,1,4096]{2,1,0:T(1,128)S(1)} async-done(((f32[8,1,4096]{2,1,0:T(1,128)}), f32[8,1,4096]{2,1,0:T(1,128)S(1)}, u32[]{:S(2)}, u32[]{:S(2)}) %all-to-all-start.2) | async-done | bytes 131104 | tf_op jit(solution)/shard_map/while/body/eval_jaxpr/all_to_all | solution.py:85
  234.4 1.3 collective-permute-start
  235.7 1.3 collective-permute-start.1
  237.1 3.4 %collective-permute-done.1 = f32[2,16,128]{2,1,0:T(8,128)S(1)} collective-permute-done((f32[2,16,128]{2,1,0:T(8,128)S(1)}, f32[2,16,128]{2,1,0:T(8,128)S(1)}, u32[]{:S(2)}, u32[]{:S(2)}) %collective-permute-start.1) | collective-permute-done | bytes 16416 | tf_op jit(solution)/shard_map/while/body/eval_jaxpr/ppermute | solution.py:21
  241.3 3.3 %all-to-all-start.1 = ((s32[8,1,2]{2,1,0:T(1,128)}), s32[8,1,2]{2,1,0:T(1,128)S(1)}, u32[]{:S(2)}, u32[]{:S(2)}) async-start(s32[8,1,2]{2,1,0:T(1,128)} %bitcast.377), calls=%async_computation.1 | async-start | bytes 8192 | tf_op jit(solution)/shard_map/while/body/eval_jaxpr/all_to_all | solution.py:71
  249.6 1.3 fusion.310
  250.9 1.3 fusion.307
  252.2 1.3 fusion.311
  253.5 1.3 fusion.309
  256.5 5.9 %all-to-all-start = ((f32[8,1,4096]{2,1,0:T(1,128)}), f32[8,1,4096]{2,1,0:T(1,128)S(1)}, u32[]{:S(2)}, u32[]{:S(2)}) async-start(f32[8,1,4096]{2,1,0:T(1,128)} %reshape.305), calls=%async_computation | async-start | bytes 262144 | tf_op jit(solution)/shard_map/while/body/eval_jaxpr/all_to_all | solution.py:70
  263.7 6.0 %all-to-all-done = f32[8,1,4096]{2,1,0:T(1,128)S(1)} async-done(((f32[8,1,4096]{2,1,0:T(1,128)}), f32[8,1,4096]{2,1,0:T(1,128)S(1)}, u32[]{:S(2)}, u32[]{:S(2)}) %all-to-all-start) | async-done | bytes 131104 | tf_op jit(solution)/shard_map/while/body/eval_jaxpr/all_to_all | solution.py:70
  275.8 3.4 %all-to-all-start.2 = ((f32[8,1,4096]{2,1,0:T(1,128)}), f32[8,1,4096]{2,1,0:T(1,128)S(1)}, u32[]{:S(2)}, u32[]{:S(2)}) async-start(f32[8,1,4096]{2,1,0:T(1,128)} %reshape.313), calls=%async_computation.2 | async-start | bytes 262144 | tf_op jit(solution)/shard_map/while/body/eval_jaxpr/all_to_all | solution.py:85
  279.2 8.2 %all-to-all-done.2 = f32[8,1,4096]{2,1,0:T(1,128)S(1)} async-done(((f32[8,1,4096]{2,1,0:T(1,128)}), f32[8,1,4096]{2,1,0:T(1,128)S(1)}, u32[]{:S(2)}, u32[]{:S(2)}) %all-to-all-start.2) | async-done | bytes 131104 | tf_op jit(solution)/shard_map/while/body/eval_jaxpr/all_to_all | solution.py:85
  293.3 1.3 collective-permute-start
  294.7 1.3 collective-permute-start.1
  296.0 3.4 %collective-permute-done.1 = f32[2,16,128]{2,1,0:T(8,128)S(1)} collective-permute-done((f32[2,16,128]{2,1,0:T(8,128)S(1)}, f32[2,16,128]{2,1,0:T(8,128)S(1)}, u32[]{:S(2)}, u32[]{:S(2)}) %collective-permute-start.1) | collective-permute-done | bytes 16416 | tf_op jit(solution)/shard_map/while/body/eval_jaxpr/ppermute | solution.py:21
  (423 shorter events, 100.1 us)
Async XLA Ops:
  0.6 0.8 copy-start.8
  0.7 0.9 copy-start.7
  0.7 0.8 copy-start.9
  0.7 0.8 copy-start.10
  1.5 10.4 %copy-start.4 = (f32[2,128,256]{2,1,0:T(8,128)S(1)}, f32[2,128,256]{2,1,0:T(8,128)}, u32[]{:S(2)}) copy-start(f32[2,128,256]{2,1,0:T(8,128)} %get-tuple-element.601) | copy-start | bytes 786436 | tf_op jit(solution)/shard_map/while
  2.4 19.1 %all-to-all-start.1 = ((s32[8,1,2]{2,1,0:T(1,128)}), s32[8,1,2]{2,1,0:T(1,128)S(1)}, u32[]{:S(2)}, u32[]{:S(2)}) async-start(s32[8,1,2]{2,1,0:T(1,128)} %bitcast.377), calls=%async_computation.1 | async-start | bytes 8192 | tf_op jit(solution)/shard_map/while/body/eval_jaxpr/all_to_all | solution.py:71
  10.7 1.5 copy-start.3
  12.1 1.1 copy-start
  12.1 2.1 copy-start.2
  21.5 13.3 %all-to-all-start = ((f32[8,1,4096]{2,1,0:T(1,128)}), f32[8,1,4096]{2,1,0:T(1,128)S(1)}, u32[]{:S(2)}, u32[]{:S(2)}) async-start(f32[8,1,4096]{2,1,0:T(1,128)} %reshape.305), calls=%async_computation | async-start | bytes 262144 | tf_op jit(solution)/shard_map/while/body/eval_jaxpr/all_to_all | solution.py:70
  36.7 1.0 copy-start.1
  40.9 10.7 %all-to-all-start.2 = ((f32[8,1,4096]{2,1,0:T(1,128)}), f32[8,1,4096]{2,1,0:T(1,128)S(1)}, u32[]{:S(2)}, u32[]{:S(2)}) async-start(f32[8,1,4096]{2,1,0:T(1,128)} %reshape.313), calls=%async_computation.2 | async-start | bytes 262144 | tf_op jit(solution)/shard_map/while/body/eval_jaxpr/all_to_all | solution.py:85
  57.5 2.6 collective-permute-start
  58.8 4.8 %collective-permute-start.1 = (f32[2,16,128]{2,1,0:T(8,128)S(1)}, f32[2,16,128]{2,1,0:T(8,128)S(1)}, u32[]{:S(2)}, u32[]{:S(2)}) collective-permute-start(f32[2,16,128]{2,1,0:T(8,128)S(1)} %get-tuple-element.542), channel_id=1, source_target_pairs={{8,0},{16,8},{24,16},{9,1},{17,9},{25,17},{10,2},{18,10},{26,18},{... | collective-permute-start | bytes 49160 | tf_op jit(solution)/shard_map/while/body/eval_jaxpr/ppermute | solution.py:21
  63.6 6.4 %copy-start.4 = (f32[2,128,256]{2,1,0:T(8,128)S(1)}, f32[2,128,256]{2,1,0:T(8,128)}, u32[]{:S(2)}) copy-start(f32[2,128,256]{2,1,0:T(8,128)} %get-tuple-element.601) | copy-start | bytes 786436 | tf_op jit(solution)/shard_map/while
  64.5 15.2 %all-to-all-start.1 = ((s32[8,1,2]{2,1,0:T(1,128)}), s32[8,1,2]{2,1,0:T(1,128)S(1)}, u32[]{:S(2)}, u32[]{:S(2)}) async-start(s32[8,1,2]{2,1,0:T(1,128)} %bitcast.377), calls=%async_computation.1 | async-start | bytes 8192 | tf_op jit(solution)/shard_map/while/body/eval_jaxpr/all_to_all | solution.py:71
  68.9 1.5 copy-start.3
  70.2 1.1 copy-start
  70.3 2.1 copy-start.2
  79.7 13.3 %all-to-all-start = ((f32[8,1,4096]{2,1,0:T(1,128)}), f32[8,1,4096]{2,1,0:T(1,128)S(1)}, u32[]{:S(2)}, u32[]{:S(2)}) async-start(f32[8,1,4096]{2,1,0:T(1,128)} %reshape.305), calls=%async_computation | async-start | bytes 262144 | tf_op jit(solution)/shard_map/while/body/eval_jaxpr/all_to_all | solution.py:70
  94.7 1.0 copy-start.1
  99.0 11.6 %all-to-all-start.2 = ((f32[8,1,4096]{2,1,0:T(1,128)}), f32[8,1,4096]{2,1,0:T(1,128)S(1)}, u32[]{:S(2)}, u32[]{:S(2)}) async-start(f32[8,1,4096]{2,1,0:T(1,128)} %reshape.313), calls=%async_computation.2 | async-start | bytes 262144 | tf_op jit(solution)/shard_map/while/body/eval_jaxpr/all_to_all | solution.py:85
  116.5 2.7 collective-permute-start
  117.9 4.7 %collective-permute-start.1 = (f32[2,16,128]{2,1,0:T(8,128)S(1)}, f32[2,16,128]{2,1,0:T(8,128)S(1)}, u32[]{:S(2)}, u32[]{:S(2)}) collective-permute-start(f32[2,16,128]{2,1,0:T(8,128)S(1)} %get-tuple-element.542), channel_id=1, source_target_pairs={{8,0},{16,8},{24,16},{9,1},{17,9},{25,17},{10,2},{18,10},{26,18},{... | collective-permute-start | bytes 49160 | tf_op jit(solution)/shard_map/while/body/eval_jaxpr/ppermute | solution.py:21
  122.6 6.4 %copy-start.4 = (f32[2,128,256]{2,1,0:T(8,128)S(1)}, f32[2,128,256]{2,1,0:T(8,128)}, u32[]{:S(2)}) copy-start(f32[2,128,256]{2,1,0:T(8,128)} %get-tuple-element.601) | copy-start | bytes 786436 | tf_op jit(solution)/shard_map/while
  123.4 15.2 %all-to-all-start.1 = ((s32[8,1,2]{2,1,0:T(1,128)}), s32[8,1,2]{2,1,0:T(1,128)S(1)}, u32[]{:S(2)}, u32[]{:S(2)}) async-start(s32[8,1,2]{2,1,0:T(1,128)} %bitcast.377), calls=%async_computation.1 | async-start | bytes 8192 | tf_op jit(solution)/shard_map/while/body/eval_jaxpr/all_to_all | solution.py:71
  127.8 1.5 copy-start.3
  129.2 1.1 copy-start
  129.2 2.1 copy-start.2
  138.6 13.3 %all-to-all-start = ((f32[8,1,4096]{2,1,0:T(1,128)}), f32[8,1,4096]{2,1,0:T(1,128)S(1)}, u32[]{:S(2)}, u32[]{:S(2)}) async-start(f32[8,1,4096]{2,1,0:T(1,128)} %reshape.305), calls=%async_computation | async-start | bytes 262144 | tf_op jit(solution)/shard_map/while/body/eval_jaxpr/all_to_all | solution.py:70
  153.7 1.0 copy-start.1
  158.0 11.6 %all-to-all-start.2 = ((f32[8,1,4096]{2,1,0:T(1,128)}), f32[8,1,4096]{2,1,0:T(1,128)S(1)}, u32[]{:S(2)}, u32[]{:S(2)}) async-start(f32[8,1,4096]{2,1,0:T(1,128)} %reshape.313), calls=%async_computation.2 | async-start | bytes 262144 | tf_op jit(solution)/shard_map/while/body/eval_jaxpr/all_to_all | solution.py:85
  175.5 2.7 collective-permute-start
  176.8 4.7 %collective-permute-start.1 = (f32[2,16,128]{2,1,0:T(8,128)S(1)}, f32[2,16,128]{2,1,0:T(8,128)S(1)}, u32[]{:S(2)}, u32[]{:S(2)}) collective-permute-start(f32[2,16,128]{2,1,0:T(8,128)S(1)} %get-tuple-element.542), channel_id=1, source_target_pairs={{8,0},{16,8},{24,16},{9,1},{17,9},{25,17},{10,2},{18,10},{26,18},{... | collective-permute-start | bytes 49160 | tf_op jit(solution)/shard_map/while/body/eval_jaxpr/ppermute | solution.py:21
  181.5 6.4 %copy-start.4 = (f32[2,128,256]{2,1,0:T(8,128)S(1)}, f32[2,128,256]{2,1,0:T(8,128)}, u32[]{:S(2)}) copy-start(f32[2,128,256]{2,1,0:T(8,128)} %get-tuple-element.601) | copy-start | bytes 786436 | tf_op jit(solution)/shard_map/while
  182.4 15.2 %all-to-all-start.1 = ((s32[8,1,2]{2,1,0:T(1,128)}), s32[8,1,2]{2,1,0:T(1,128)S(1)}, u32[]{:S(2)}, u32[]{:S(2)}) async-start(s32[8,1,2]{2,1,0:T(1,128)} %bitcast.377), calls=%async_computation.1 | async-start | bytes 8192 | tf_op jit(solution)/shard_map/while/body/eval_jaxpr/all_to_all | solution.py:71
  186.8 1.5 copy-start.3
  188.1 1.1 copy-start
  188.1 2.1 copy-start.2
  197.6 13.3 %all-to-all-start = ((f32[8,1,4096]{2,1,0:T(1,128)}), f32[8,1,4096]{2,1,0:T(1,128)S(1)}, u32[]{:S(2)}, u32[]{:S(2)}) async-start(f32[8,1,4096]{2,1,0:T(1,128)} %reshape.305), calls=%async_computation | async-start | bytes 262144 | tf_op jit(solution)/shard_map/while/body/eval_jaxpr/all_to_all | solution.py:70
  212.6 1.0 copy-start.1
  216.9 11.6 %all-to-all-start.2 = ((f32[8,1,4096]{2,1,0:T(1,128)}), f32[8,1,4096]{2,1,0:T(1,128)S(1)}, u32[]{:S(2)}, u32[]{:S(2)}) async-start(f32[8,1,4096]{2,1,0:T(1,128)} %reshape.313), calls=%async_computation.2 | async-start | bytes 262144 | tf_op jit(solution)/shard_map/while/body/eval_jaxpr/all_to_all | solution.py:85
  234.4 2.7 collective-permute-start
  235.7 4.7 %collective-permute-start.1 = (f32[2,16,128]{2,1,0:T(8,128)S(1)}, f32[2,16,128]{2,1,0:T(8,128)S(1)}, u32[]{:S(2)}, u32[]{:S(2)}) collective-permute-start(f32[2,16,128]{2,1,0:T(8,128)S(1)} %get-tuple-element.542), channel_id=1, source_target_pairs={{8,0},{16,8},{24,16},{9,1},{17,9},{25,17},{10,2},{18,10},{26,18},{... | collective-permute-start | bytes 49160 | tf_op jit(solution)/shard_map/while/body/eval_jaxpr/ppermute | solution.py:21
  240.4 6.4 %copy-start.4 = (f32[2,128,256]{2,1,0:T(8,128)S(1)}, f32[2,128,256]{2,1,0:T(8,128)}, u32[]{:S(2)}) copy-start(f32[2,128,256]{2,1,0:T(8,128)} %get-tuple-element.601) | copy-start | bytes 786436 | tf_op jit(solution)/shard_map/while
  241.3 15.2 %all-to-all-start.1 = ((s32[8,1,2]{2,1,0:T(1,128)}), s32[8,1,2]{2,1,0:T(1,128)S(1)}, u32[]{:S(2)}, u32[]{:S(2)}) async-start(s32[8,1,2]{2,1,0:T(1,128)} %bitcast.377), calls=%async_computation.1 | async-start | bytes 8192 | tf_op jit(solution)/shard_map/while/body/eval_jaxpr/all_to_all | solution.py:71
  245.7 1.5 copy-start.3
  247.1 1.1 copy-start
  247.1 2.1 copy-start.2
  256.5 13.3 %all-to-all-start = ((f32[8,1,4096]{2,1,0:T(1,128)}), f32[8,1,4096]{2,1,0:T(1,128)S(1)}, u32[]{:S(2)}, u32[]{:S(2)}) async-start(f32[8,1,4096]{2,1,0:T(1,128)} %reshape.305), calls=%async_computation | async-start | bytes 262144 | tf_op jit(solution)/shard_map/while/body/eval_jaxpr/all_to_all | solution.py:70
  271.6 1.0 copy-start.1
  275.8 11.6 %all-to-all-start.2 = ((f32[8,1,4096]{2,1,0:T(1,128)}), f32[8,1,4096]{2,1,0:T(1,128)S(1)}, u32[]{:S(2)}, u32[]{:S(2)}) async-start(f32[8,1,4096]{2,1,0:T(1,128)} %reshape.313), calls=%async_computation.2 | async-start | bytes 262144 | tf_op jit(solution)/shard_map/while/body/eval_jaxpr/all_to_all | solution.py:85
  293.3 2.7 collective-permute-start
  294.7 4.7 %collective-permute-start.1 = (f32[2,16,128]{2,1,0:T(8,128)S(1)}, f32[2,16,128]{2,1,0:T(8,128)S(1)}, u32[]{:S(2)}, u32[]{:S(2)}) collective-permute-start(f32[2,16,128]{2,1,0:T(8,128)S(1)} %get-tuple-element.542), channel_id=1, source_target_pairs={{8,0},{16,8},{24,16},{9,1},{17,9},{25,17},{10,2},{18,10},{26,18},{... | collective-permute-start | bytes 49160 | tf_op jit(solution)/shard_map/while/body/eval_jaxpr/ppermute | solution.py:21
  299.4 0.6 copy-start.5
  299.4 0.6 copy-start.6
where the time goes:
time: 304 us; the launch traced here: 300 us
  waiting for transfers between devices  87 us (29%)
  starting transfers between devices  80.3 us (26%)
  matrix products  80.3 us (26%)
  local copies, waits for them, and re-layouts  33.8 us (11%)
  other arithmetic  15.3 us (5%)
    all_to_all x5, waiting for transfers between devices, front_solve(): lax.all_to_all(reply, 'front', split_axis=0, concat_axis=0, tiled=True)  40.1 us
    all_to_all x5, waiting for transfers between devices, front_solve(): lax.all_to_all(outgoing, 'front', split_axis=0, concat_axis=0, tiled=True)  30 us
    all_to_all x5, starting transfers between devices, front_solve(): lax.all_to_all(outgoing, 'front', split_axis=0, concat_axis=0, tiled=True)  29.6 us
    dot_general x35, matrix products, complex_product(): jnp.einsum(pattern, first[0], second[0], precision=precise)  20.6 us
    all_to_all x5, starting transfers between devices, front_solve(): lax.all_to_all(slot_offset, 'front', split_axis=0, concat_axis=0, tiled=T...  20.5 us
    dot_general x35, matrix products, complex_product(): jnp.einsum(pattern, first[0], second[1], precision=precise)  20.3 us
    all_to_all x5, starting transfers between devices, front_solve(): lax.all_to_all(reply, 'front', split_axis=0, concat_axis=0, tiled=True)  17 us
    ppermute x10, waiting for transfers between devices, passed_along(): lax.ppermute(value, axis, [(source, source + steps) for source in range(i...  16.9 us
  transfers between devices with their start and end apart: 25, of which 15 were waited for; matrix products, arithmetic and copies ran while one was open for 21% of the time, Pallas kernels for 0%

commit v1 on v0

v1 whole, which is shorter than its diff:
```python
import functools

import jax
import jax.numpy as jnp
from jax import lax
from jax.experimental import pallas as pl
from jax.experimental.pallas import tpu as pltpu
from jax.sharding import PartitionSpec as P

CAP = 2
F32 = jnp.float32
BF16 = jnp.bfloat16


def split(x):
    hi = x.astype(BF16)
    return hi, (x - hi.astype(F32)).astype(BF16)


def mm(a, b, rhs_dim=0):
    return lax.dot_general(a, b, (((1,), (rhs_dim,)), ((), ())), preferred_element_type=F32)


def dot3(a, b, rhs_dim=0):
    return mm(a[0], b[0], rhs_dim) + (mm(a[0], b[1], rhs_dim) + mm(a[1], b[0], rhs_dim))


def turned(x):
    half = x.shape[1] // 2
    return jnp.concatenate([-x[:, half:], x[:, :half]], axis=1)


def apply(w_hi, w_lo, x):
    n = x.shape[1]
    hi, lo = split(jnp.concatenate([x, turned(x)], axis=0))
    p = mm(w_hi, jnp.concatenate([hi, lo], axis=1))
    return p[:, :n] + p[:, n:] + mm(w_lo, hi)


def twin(cat):
    half = cat.shape[1] // 2
    re, im = cat[:, :half], cat[:, half:]
    return jnp.concatenate(
        [jnp.concatenate([re, -im], axis=1), jnp.concatenate([im, re], axis=1)], axis=0
    )


def kernel(
    leaves, depth,
    tgt, off, s_down, s_up, leaf, coup, sep, j_top, j_bot,
    out_down, out_up,
    lw, cw, sw, jw, m1, m2, ybuf, ubuf, msend, marr, usend, uarr, rsend, rarr, tsend, tarr,
    ms, mr, us, ur, rs, rr, ts, tr,
):
    layer, me = lax.axis_index("layer"), lax.axis_index("front")
    nb, rb, psize = coup.shape[1:]
    qsize = sep.shape[1]
    qb = qsize // rb
    cols = s_down.shape[1]
    tsize = j_top.shape[1]
    lanes = 2 * cols
    width = CAP * lanes
    slots = leaves * CAP

    barrier = pltpu.get_barrier_semaphore()
    for i in range(1, leaves):
        pl.semaphore_signal(
            barrier, inc=1, device_id={"front": lax.rem(me + i, leaves)}, device_id_type=pl.DeviceIdType.MESH
        )
    inward, onward = layer > 0, layer < depth - 1
    inner = jnp.logical_and(inward, onward)

    @pl.when(inward)
    def _():
        pl.semaphore_signal(barrier, inc=1, device_id={"layer": layer - 1}, device_id_type=pl.DeviceIdType.MESH)

    @pl.when(onward)
    def _():
        pl.semaphore_signal(barrier, inc=1, device_id={"layer": layer + 1}, device_id_type=pl.DeviceIdType.MESH)

    first = lax.div(2 * layer, depth)
    way = (first, 1 - first)

    t = [tgt[n] for n in range(nb)]
    o = [off[n] for n in range(nb)]
    slot = []
    for n in range(nb):
        rank = jnp.int32(0)
        for m in range(n):
            rank = rank + jnp.where(t[m] == t[n], 1, 0)
        slot.append(t[n] * CAP + rank)
    lane = lax.broadcasted_iota(jnp.int32, (qb, width), 1)
    row = lax.broadcasted_iota(jnp.int32, (qb, width), 0)
    for p in range(2):
        hi, lo = split(leaf[p])
        lw[0, :, p * psize:(p + 1) * psize] = hi
        lw[1, :, p * psize:(p + 1) * psize] = lo
    for s in range(leaves):
        place = jnp.full((qb, width), -1, jnp.int32)
        for c in range(CAP):
            k = s * CAP + c
            block, count, where = jnp.int32(0), jnp.int32(0), jnp.int32(0)
            for n in range(nb):
                hit = slot[n] == k
                block = block + jnp.where(hit, n, 0)
                count = count + jnp.where(hit, 1, 0)
                where = where + jnp.where(hit, o[n], 0)
            where = jnp.where(count > 0, where, -1)
            place = jnp.where(lax.div(lane, lanes) == c, where, place)
            keep = count.astype(F32)
            for p in range(2):
                hi, lo = split(coup[p, block] * keep)
                cw[0, k * rb:(k + 1) * rb, p * psize:(p + 1) * psize] = hi
                cw[1, k * rb:(k + 1) * rb, p * psize:(p + 1) * psize] = lo
        msend[s] = jnp.where(row == place, 1.0, 0.0).astype(F32)
    marr[me] = msend[me]

    def prepare(e):
        up = way[e] > 0
        g = jnp.where(up, s_up[...], s_down[...]).reshape(2 * cols, psize).T
        y = apply(lw[0], lw[1], g)
        ybuf[e] = y
        ubuf[e] = apply(cw[0], cw[1], y)

    prepare(0)

    def across(src, dst, send, recv, i, tag):
        there, back = lax.rem(me + i, leaves), lax.rem(me + leaves - i, leaves)
        kind = pl.DeviceIdType.MESH
        out = pltpu.make_async_remote_copy(
            src.at[tag + (there,)], dst.at[tag + (me,)], send.at[tag + (there,)], recv.at[tag + (me,)],
            device_id={"front": there}, device_id_type=kind)
        into = pltpu.make_async_remote_copy(
            src.at[tag + (back,)], dst.at[tag + (back,)], send.at[tag + (back,)], recv.at[tag + (back,)],
            device_id={"front": back}, device_id_type=kind)
        return out, into

    mask_moves = [across(msend, marr, ms, mr, i, ()) for i in range(1, leaves)]
    u_moves = [[across(usend, uarr, us, ur, i, (e,)) for i in range(1, leaves)] for e in range(2)]
    r_moves = [[across(rsend, rarr, rs, rr, i, (e,)) for i in range(1, leaves)] for e in range(2)]

    def trace_move(e):
        d = way[e]
        return pltpu.make_async_remote_copy(
            tsend.at[d], tarr.at[d], ts.at[d], tr.at[d],
            device_id={"layer": layer + 1 - 2 * d}, device_id_type=pl.DeviceIdType.MESH)

    def arrived_trace(e):
        d = way[e]
        pltpu.make_async_remote_copy(
            tsend.at[d], tarr.at[d], ts.at[d], tr.at[d],
            device_id={"layer": layer - 1 + 2 * d}, device_id_type=pl.DeviceIdType.MESH).wait_recv()
        held = tarr[d]
        return jnp.concatenate([held[:, :lanes], held[:, lanes:]], axis=0)

    def send_update(e, u):
        for s in range(leaves):
            usend[e, s] = jnp.concatenate(
                [u[(s * CAP + c) * rb:(s * CAP + c + 1) * rb] for c in range(CAP)], axis=1)
        for out, _ in u_moves[e]:
            out.start()
        uarr[e, me] = usend[e, me]

    def with_trace(e):
        d = way[e]
        trace = arrived_trace(e)
        send_update(e, ubuf[e] + apply(m1[0, d], m1[1, d], trace))
        ybuf[e] = ybuf[e] + apply(jw[0, d], jw[1, d], trace)

    pl.semaphore_wait(barrier, leaves - 1 + jnp.where(inward, 1, 0) + jnp.where(onward, 1, 0))
    for out, _ in mask_moves:
        out.start()

    @pl.when(jnp.logical_not(inner))
    def _():
        send_update(0, ubuf[0])

    for p in range(2):
        hi, lo = split(sep[p])
        sw[0, :, p * qsize:(p + 1) * qsize] = hi
        sw[1, :, p * qsize:(p + 1) * qsize] = lo
    for d, inject in enumerate((j_top, j_bot)):
        mapping = twin(jnp.concatenate([inject[0], inject[1]], axis=1))
        lj = dot3((lw[0], lw[1]), split(mapping), 1)
        jw[0, d], jw[1, d] = split(lj)
        ljr, lji = lj[:, :tsize], lj[:, tsize:]
        grid = jnp.concatenate(
            [jnp.concatenate([ljr, lji], axis=1), jnp.concatenate([-lji, ljr], axis=1)], axis=0)
        m1[0, d], m1[1, d] = split(dot3((cw[0], cw[1]), split(grid)))

    @pl.when(inner)
    def _():
        with_trace(0)

    for e in range(2):
        d = way[e]
        if e == 1:
            with_trace(1)
        else:
            for _, into in mask_moves:
                into.wait_recv()
        for _, into in u_moves[e]:
            into.wait_recv()
        blocks = []
        for b in range(qb):
            total = uarr[e, 0] * marr[0, b:b + 1]
            for s in range(1, leaves):
                total = total + uarr[e, s] * marr[s, b:b + 1]
            part = total[:, :lanes]
            for c in range(1, CAP):
                part = part + total[:, c * lanes:(c + 1) * lanes]
            blocks.append(part)
        x = apply(sw[0], sw[1], jnp.concatenate(blocks, axis=0))
        wide = [jnp.concatenate([x[b * rb:(b + 1) * rb]] * CAP, axis=1) for b in range(qb)]
        for s in range(leaves):
            total = wide[0] * marr[s, 0:1]
            for b in range(1, qb):
                total = total + wide[b] * marr[s, b:b + 1]
            rsend[e, s] = total
        for out, _ in r_moves[e]:
            out.start()
        rarr[e, me] = rsend[e, me]
        if e == 0:
            chi, clo = twin(cw[0]), twin(cw[1])
            m2[0], m2[1] = split(dot3((lw[0], lw[1]), (chi, clo), 1))
            prepare(1)
        for _, into in r_moves[e]:
            into.wait_recv()
        w = jnp.concatenate(
            [rarr[e, s][:, c * lanes:(c + 1) * lanes] for s in range(leaves) for c in range(CAP)], axis=0)

        def pass_on():
            rows = pl.ds(pl.multiple_of((1 - d) * (psize - tsize), 8), tsize)
            trace = ybuf[e, rows] + apply(m2[0, rows], m2[1, rows], w)
            tsend[d] = jnp.concatenate([trace[:tsize // 2], trace[tsize // 2:]], axis=1)
            trace_move(e).start()

        if e == 0:
            pass_on()
        else:
            pl.when(inner)(pass_on)
        field = (ybuf[e] + apply(m2[0], m2[1], w)).T.reshape(2, cols, psize)

        @pl.when(d == 0)
        def _():
            out_down[...] = field

        @pl.when(d == 1)
        def _():
            out_up[...] = field

    for moves in [mask_moves] + u_moves + r_moves:
        for out, _ in moves:
            out.wait_send()
    trace_move(0).wait_send()

    @pl.when(inner)
    def _():
        trace_move(1).wait_send()


def solution(mesh):
    leaves, depth = mesh.shape["front"], mesh.shape["layer"]

    def body(s_down, s_up, leaf, coup, sep, j_top, j_bot, targets, offsets):
        cols, psize = s_down.shape[3:]
        nb = offsets.shape[2]
        bsize, qsize, tsize = coup.shape[3], sep.shape[3], j_top.shape[3]
        rb = bsize // nb
        qb = qsize // rb
        lanes = 2 * cols
        width = CAP * lanes
        rows = leaves * CAP * rb
        vmem = pl.BlockSpec(memory_space=pltpu.VMEM)
        smem = pl.BlockSpec(memory_space=pltpu.SMEM)
        sems = pltpu.SemaphoreType.DMA
        field = jax.ShapeDtypeStruct((2, cols, psize), F32)
        down, up = pl.pallas_call(
            functools.partial(kernel, leaves, depth),
            out_shape=(field, field),
            in_specs=[smem] * 2 + [vmem] * 7,
            out_specs=(vmem, vmem),
            scratch_shapes=[
                pltpu.VMEM((2, psize, 2 * psize), BF16),
                pltpu.VMEM((2, rows, 2 * psize), BF16),
                pltpu.VMEM((2, qsize, 2 * qsize), BF16),
                pltpu.VMEM((2, 2, psize, 2 * tsize), BF16),
                pltpu.VMEM((2, 2, rows, 2 * tsize), BF16),
                pltpu.VMEM((2, psize, 2 * rows), BF16),
                pltpu.VMEM((2, psize, lanes), F32),
                pltpu.VMEM((2, rows, lanes), F32),
                pltpu.VMEM((leaves, qb, width), F32),
                pltpu.VMEM((leaves, qb, width), F32),
                pltpu.VMEM((2, leaves, rb, width), F32),
                pltpu.VMEM((2, leaves, rb, width), F32),
                pltpu.VMEM((2, leaves, rb, width), F32),
                pltpu.VMEM((2, leaves, rb, width), F32),
                pltpu.VMEM((2, tsize // 2, 2 * lanes), F32),
                pltpu.VMEM((2, tsize // 2, 2 * lanes), F32),
                sems((leaves,)), sems((leaves,)),
                sems((2, leaves)), sems((2, leaves)),
                sems((2, leaves)), sems((2, leaves)),
                sems((2,)), sems((2,)),
            ],
            compiler_params=pltpu.CompilerParams(
                collective_id=0, has_side_effects=True, vmem_limit_bytes=56 * 1024 * 1024
            ),
        )(
            targets.reshape(nb), offsets.reshape(nb),
            s_down[0, 0], s_up[0, 0], leaf[0, 0], coup[0, 0].reshape(2, nb, rb, psize),
            sep[0, 0], j_top[0, 0], j_bot[0, 0],
        )
        return down[None, None], up[None, None]

    five, four, three = (P("layer", "front", *([None] * k)) for k in (3, 2, 1))
    return jax.shard_map(
        body, mesh=mesh, in_specs=(five,) * 7 + (four, three), out_specs=(five, five), check_vma=False
    )
```

time: 304 us -> 56.8 us (0.19); the launches traced: 300 us -> 56.6 us
  waiting for transfers between devices: 87 us -> 0 us
  matrix products: 80.3 us -> 0 us
  starting transfers between devices: 80.3 us -> 0 us
  Pallas kernels: 0 us -> 53.8 us
  local copies, waits for them, and re-layouts: 33.8 us -> 2.14 us
  other arithmetic: 15.3 us -> 0 us
    dot_general x160 -> x0, matrix products: 80.3 us -> none  [the longest x35 20.6 us: complex_product(): jnp.einsum(pattern, first[0], second[0], precision=precise)]
    all_to_all x15 -> x0, waiting for transfers between devices: 70.1 us -> none  [the longest x5 40.1 us: front_solve(): lax.all_to_all(reply, 'front', split_axis=0, concat_axis=0, tiled=True)]
    all_to_all x15 -> x0, starting transfers between devices: 67.2 us -> none  [the longest x5 29.6 us: front_solve(): lax.all_to_all(outgoing, 'front', split_axis=0, concat_axis=0, tiled=True)]
    pallas_call x0 -> x1, Pallas kernels: none -> 53.8 us  [body(): pl.pallas_call(functools.partial(kernel, leaves, depth), out_shape=(field...]
    ppermute x10 -> x0, waiting for transfers between devices: 16.9 us -> none  [passed_along(): lax.ppermute(value, axis, [(source, source + steps) for source in range(i...]
    ppermute x10 -> x0, starting transfers between devices: 13.1 us -> none  [passed_along(): lax.ppermute(value, axis, [(source, source + steps) for source in range(i...]
    all_to_all x15 -> x0, other arithmetic: 12.9 us -> none  [the longest x5 4.8 us: front_solve(): lax.all_to_all(outgoing, 'front', split_axis=0, concat_axis=0, tiled=True)]
    while x70 -> x0, local copies, waits for them, and re-layouts: 12.3 us -> none
  transfers between devices with their start and end apart: 25 -> 0, of which waited for: 15 -> 0; matrix products, arithmetic and copies ran while one was open for 21% -> 0% of each run, Pallas kernels for 0% -> 0%
where the time goes in v1:
time: 56.8 us; the launch traced here: 56.6 us
  Pallas kernels  53.8 us (95%)
  local copies, waits for them, and re-layouts  2.14 us (4%)
  between operations  0.65 us (1%)
    pallas_call x1, Pallas kernels, body(): pl.pallas_call(functools.partial(kernel, leaves, depth), out_shape=(field...  53.8 us
    unnamed x4, local copies, waits for them, and re-layouts  2.14 us

profile of v1, /device:TPU:0, one launch (start us, length us, event | category | flops | bytes accessed | tf_op | source)
XLA Modules:
  0.0 56.6 jit_solution(1854698376710888531)
XLA Ops:
  0.6 53.8 %shard_map.104 = (f32[2,32,256]{2,1,0:T(8,128)}, f32[2,32,256]{2,1,0:T(8,128)}) custom-call(s32[16]{0:T(128)} %bitcast.20, s32[16]{0:T(128)} %bitcast.21, f32[2,32,256]{2,1,0:T(8,128)} %bitcast.16, f32[2,32,256]{2,1,0:T(8,128)} %bitcast.17, f32[2,256,256]{2,1,0:T(8,128)} %bitcast.12, f32[2,16,32,256]{3,2,1,0:T(8,128)} %bitcast.11, f32[2,256,256]{2,1,0:T(8,128)} %bitcast.13, ...), custom_call_target="tpu_custom_call" | custom-call | tf_op jit(solution)/shard_map/pallas_call | solution.py:278
  54.4 0.0 copy-start
  54.4 1.5 %copy.13 = f32[1,1,2,32,256]{4,3,2,1,0:T(8,128)} copy(f32[1,1,2,32,256]{4,3,2,1,0:T(8,128)} %bitcast.19) | data formatting | bytes 131072
  56.0 0.0 copy-done
  56.0 0.6 %copy.14 = f32[1,1,2,32,256]{4,3,2,1,0:T(8,128)} copy(f32[1,1,2,32,256]{4,3,2,1,0:T(8,128)S(1)} %bitcast.18) | data formatting | bytes 131072
Async XLA Ops:
  54.4 1.5 %copy-start = (f32[2,32,256]{2,1,0:T(8,128)S(1)}, f32[2,32,256]{2,1,0:T(8,128)}, u32[]{:S(2)}) copy-start(f32[2,32,256]{2,1,0:T(8,128)} %get-tuple-element.5) | copy-start | bytes 196612

commit v2 on v1

--- a/solution.py
+++ b/solution.py
@@ -25,16 +25,35 @@
     return mm(a[0], b[0], rhs_dim) + (mm(a[0], b[1], rhs_dim) + mm(a[1], b[0], rhs_dim))
 
 
-def turned(x):
-    half = x.shape[1] // 2
-    return jnp.concatenate([-x[:, half:], x[:, :half]], axis=1)
-
-
-def apply(w_hi, w_lo, x):
+def lanes_of(x):
+    return lax.broadcasted_iota(jnp.int32, x.shape, 1)
+
+
+def turned(x, cols):
+    real = lax.rem(lanes_of(x), 2 * cols) < cols
+    return jnp.where(real, -pltpu.roll(x, x.shape[1] - cols, 1), pltpu.roll(x, cols, 1))
+
+
+def apply(w_hi, w_lo, x, cols):
     n = x.shape[1]
-    hi, lo = split(jnp.concatenate([x, turned(x)], axis=0))
+    hi, lo = split(jnp.concatenate([x, turned(x, cols)], axis=0))
     p = mm(w_hi, jnp.concatenate([hi, lo], axis=1))
     return p[:, :n] + p[:, n:] + mm(w_lo, hi)
+
+
+def pick(parts, group):
+    which = lax.div(lanes_of(parts[0]), group)
+    out = parts[0]
+    for c in range(1, len(parts)):
+        out = jnp.where(which == c, parts[c], out)
+    return out
+
+
+def folded(x, group):
+    out = x
+    for c in range(1, x.shape[1] // group):
+        out = out + pltpu.roll(x, c * group, 1)
+    return out
 
 
 def twin(cat):
@@ -47,11 +66,18 @@
 
 def kernel(
     leaves, depth,
-    tgt, off, s_down, s_up, leaf, coup, sep, j_top, j_bot,
+    tgt, off, s_down, s_up, leaf, coup, sep_far, top_far, bot_far,
     out_down, out_up,
+    sep, j_top, j_bot,
     lw, cw, sw, jw, m1, m2, ybuf, ubuf, msend, marr, usend, uarr, rsend, rarr, tsend, tarr,
-    ms, mr, us, ur, rs, rr, ts, tr,
+    ls, ms, mr, us, ur, rs, rr, ts, tr,
 ):
+    loads = [
+        pltpu.make_async_copy(far, near, ls.at[i])
+        for i, (far, near) in enumerate(((sep_far, sep), (top_far, j_top), (bot_far, j_bot)))
+    ]
+    for load in loads:
+        load.start()
     layer, me = lax.axis_index("layer"), lax.axis_index("front")
     nb, rb, psize = coup.shape[1:]
     qsize = sep.shape[1]
@@ -60,7 +86,8 @@
     tsize = j_top.shape[1]
     lanes = 2 * cols
     width = CAP * lanes
-    slots = leaves * CAP
+    wide = leaves * rb
+    apply_c = functools.partial(apply, cols=cols)
 
     barrier = pltpu.get_barrier_semaphore()
     for i in range(1, leaves):
@@ -98,7 +125,7 @@
     for s in range(leaves):
         place = jnp.full((qb, width), -1, jnp.int32)
         for c in range(CAP):
-            k = s * CAP + c
+            k, at = s * CAP + c, c * leaves + s
             block, count, where = jnp.int32(0), jnp.int32(0), jnp.int32(0)
             for n in range(nb):
                 hit = slot[n] == k
@@ -110,22 +137,28 @@
             keep = count.astype(F32)
             for p in range(2):
                 hi, lo = split(coup[p, block] * keep)
-                cw[0, k * rb:(k + 1) * rb, p * psize:(p + 1) * psize] = hi
-                cw[1, k * rb:(k + 1) * rb, p * psize:(p + 1) * psize] = lo
+                cw[0, at * rb:(at + 1) * rb, p * psize:(p + 1) * psize] = hi
+                cw[1, at * rb:(at + 1) * rb, p * psize:(p + 1) * psize] = lo
         msend[s] = jnp.where(row == place, 1.0, 0.0).astype(F32)
     marr[me] = msend[me]
 
+    def packed(u):
+        return pick([u[c * wide:(c + 1) * wide] for c in range(CAP)], lanes)
+
     def prepare(e):
         up = way[e] > 0
-        g = jnp.where(up, s_up[...], s_down[...]).reshape(2 * cols, psize).T
-        y = apply(lw[0], lw[1], g)
+        g = jnp.where(up, s_up[...], s_down[...]).reshape(lanes, psize)
+        y = apply_c(lw[0], lw[1], jnp.concatenate([g] * CAP, axis=0).T)
         ybuf[e] = y
-        ubuf[e] = apply(cw[0], cw[1], y)
+        ubuf[e] = packed(apply_c(cw[0], cw[1], y))
 
     prepare(0)
 
+    side = 2 * lax.div(2 * me, leaves) - 1
+
     def across(src, dst, send, recv, i, tag):
-        there, back = lax.rem(me + i, leaves), lax.rem(me + leaves - i, leaves)
+        there = lax.rem(me + leaves + side * i, leaves)
+        back = there
         kind = pl.DeviceIdType.MESH
         out = pltpu.make_async_remote_copy(
             src.at[tag + (there,)], dst.at[tag + (me,)], send.at[tag + (there,)], recv.at[tag + (me,)],
@@ -151,12 +184,11 @@
             tsend.at[d], tarr.at[d], ts.at[d], tr.at[d],
             device_id={"layer": layer - 1 + 2 * d}, device_id_type=pl.DeviceIdType.MESH).wait_recv()
         held = tarr[d]
-        return jnp.concatenate([held[:, :lanes], held[:, lanes:]], axis=0)
+        over = pltpu.roll(held, lanes, 1)
+        return jnp.concatenate([pick([held, over], lanes), pick([over, held], lanes)], axis=0)
 
     def send_update(e, u):
-        for s in range(leaves):
-            usend[e, s] = jnp.concatenate(
-                [u[(s * CAP + c) * rb:(s * CAP + c + 1) * rb] for c in range(CAP)], axis=1)
+        usend[e] = u.reshape(leaves, rb, width)
         for out, _ in u_moves[e]:
             out.start()
         uarr[e, me] = usend[e, me]
@@ -164,8 +196,8 @@
     def with_trace(e):
         d = way[e]
         trace = arrived_trace(e)
-        send_update(e, ubuf[e] + apply(m1[0, d], m1[1, d], trace))
-        ybuf[e] = ybuf[e] + apply(jw[0, d], jw[1, d], trace)
+        send_update(e, ubuf[e] + packed(apply_c(m1[0, d], m1[1, d], trace)))
+        ybuf[e] = ybuf[e] + apply_c(jw[0, d], jw[1, d], trace)
 
     pl.semaphore_wait(barrier, leaves - 1 + jnp.where(inward, 1, 0) + jnp.where(onward, 1, 0))
     for out, _ in mask_moves:
@@ -175,6 +207,8 @@
     def _():
         send_update(0, ubuf[0])
 
+    for load in loads:
+        load.wait()
     for p in range(2):
         hi, lo = split(sep[p])
         sw[0, :, p * qsize:(p + 1) * qsize] = hi
@@ -199,47 +233,54 @@
         else:
             for _, into in mask_moves:
                 into.wait_recv()
-        for _, into in u_moves[e]:
-            into.wait_recv()
-        blocks = []
-        for b in range(qb):
-            total = uarr[e, 0] * marr[0, b:b + 1]
-            for s in range(1, leaves):
-                total = total + uarr[e, s] * marr[s, b:b + 1]
-            part = total[:, :lanes]
-            for c in range(1, CAP):
-                part = part + total[:, c * lanes:(c + 1) * lanes]
-            blocks.append(part)
-        x = apply(sw[0], sw[1], jnp.concatenate(blocks, axis=0))
-        wide = [jnp.concatenate([x[b * rb:(b + 1) * rb]] * CAP, axis=1) for b in range(qb)]
+        total = [uarr[e, me] * marr[me, b:b + 1] for b in range(qb)]
+        for i in range(leaves - 1, 0, -1):
+            u_moves[e][i - 1][1].wait_recv()
+            there = lax.rem(me + leaves + side * i, leaves)
+            came, mask = uarr[e, there], marr[there]
+            total = [total[b] + came * mask[b:b + 1] for b in range(qb)]
+        x = apply_c(sw[0], sw[1], jnp.concatenate([folded(part, lanes) for part in total], axis=0))
         for s in range(leaves):
-            total = wide[0] * marr[s, 0:1]
+            reply = x[:rb] * marr[s, 0:1]
             for b in range(1, qb):
-                total = total + wide[b] * marr[s, b:b + 1]
-            rsend[e, s] = total
+                reply = reply + x[b * rb:(b + 1) * rb] * marr[s, b:b + 1]
+            rsend[e, s] = reply
         for out, _ in r_moves[e]:
             out.start()
         rarr[e, me] = rsend[e, me]
         if e == 0:
             chi, clo = twin(cw[0]), twin(cw[1])
-            m2[0], m2[1] = split(dot3((lw[0], lw[1]), (chi, clo), 1))
+            full = split(dot3((lw[0], lw[1]), (chi, clo), 1))
+            for part in range(2):
+                for c in range(CAP):
+                    for p in range(2):
+                        begin = (p * CAP + c) * wide
+                        m2[part, c, :, p * wide:(p + 1) * wide] = full[part][:, begin:begin + wide]
             prepare(1)
         for _, into in r_moves[e]:
             into.wait_recv()
-        w = jnp.concatenate(
-            [rarr[e, s][:, c * lanes:(c + 1) * lanes] for s in range(leaves) for c in range(CAP)], axis=0)
+        w = rarr[e].reshape(wide, width)
+        w_hi, w_lo = split(jnp.concatenate([w, turned(w, cols)], axis=0))
+        w_both = jnp.concatenate([w_hi, w_lo], axis=1)
+
+        def corrected(rows):
+            parts = []
+            for c in range(CAP):
+                p = mm(m2[0, c, rows], w_both)
+                parts.append(p[:, :width] + p[:, width:] + mm(m2[1, c, rows], w_hi))
+            return ybuf[e, rows] + folded(pick(parts, lanes), lanes)
 
         def pass_on():
             rows = pl.ds(pl.multiple_of((1 - d) * (psize - tsize), 8), tsize)
-            trace = ybuf[e, rows] + apply(m2[0, rows], m2[1, rows], w)
-            tsend[d] = jnp.concatenate([trace[:tsize // 2], trace[tsize // 2:]], axis=1)
+            trace = corrected(rows)
+            tsend[d] = pick([trace[:tsize // 2], trace[tsize // 2:]], lanes)
             trace_move(e).start()
 
         if e == 0:
             pass_on()
         else:
             pl.when(inner)(pass_on)
-        field = (ybuf[e] + apply(m2[0], m2[1], w)).T.reshape(2, cols, psize)
+        field = corrected(pl.ds(0, psize)).T[:lanes].reshape(2, cols, psize)
 
         @pl.when(d == 0)
         def _():
@@ -278,17 +319,20 @@
         down, up = pl.pallas_call(
             functools.partial(kernel, leaves, depth),
             out_shape=(field, field),
-            in_specs=[smem] * 2 + [vmem] * 7,
+            in_specs=[smem] * 2 + [vmem] * 4 + [pl.BlockSpec(memory_space=pl.ANY)] * 3,
             out_specs=(vmem, vmem),
             scratch_shapes=[
+                pltpu.VMEM((2, qsize, qsize), F32),
+                pltpu.VMEM((2, tsize, psize), F32),
+                pltpu.VMEM((2, tsize, psize), F32),
                 pltpu.VMEM((2, psize, 2 * psize), BF16),
                 pltpu.VMEM((2, rows, 2 * psize), BF16),
                 pltpu.VMEM((2, qsize, 2 * qsize), BF16),
                 pltpu.VMEM((2, 2, psize, 2 * tsize), BF16),
                 pltpu.VMEM((2, 2, rows, 2 * tsize), BF16),
-                pltpu.VMEM((2, psize, 2 * rows), BF16),
-                pltpu.VMEM((2, psize, lanes), F32),
-                pltpu.VMEM((2, rows, lanes), F32),
+                pltpu.VMEM((2, CAP, psize, 2 * leaves * rb), BF16),
+                pltpu.VMEM((2, psize, width), F32),
+                pltpu.VMEM((2, leaves * rb, width), F32),
                 pltpu.VMEM((leaves, qb, width), F32),
                 pltpu.VMEM((leaves, qb, width), F32),
                 pltpu.VMEM((2, leaves, rb, width), F32),
@@ -297,6 +341,7 @@
                 pltpu.VMEM((2, leaves, rb, width), F32),
                 pltpu.VMEM((2, tsize // 2, 2 * lanes), F32),
                 pltpu.VMEM((2, tsize // 2, 2 * lanes), F32),
+                sems((3,)),
                 sems((leaves,)), sems((leaves,)),
                 sems((2, leaves)), sems((2, leaves)),
                 sems((2, leaves)), sems((2, leaves)),

time: 56.8 us -> 53.3 us (0.938)
  Pallas kernels: 53.8 us -> 50.3 us
    pallas_call x1, Pallas kernels: 53.8 us -> 50.3 us  [body(): pl.pallas_call(functools.partial(kernel, leaves, depth), out_shape=(field...]
where the time goes in v2:
time: 53.3 us; the launch traced here: 53.1 us
  Pallas kernels  50.3 us (94%)
  local copies, waits for them, and re-layouts  2.14 us (4%)
  between operations  0.65 us (1%)
    pallas_call x1, Pallas kernels, body(): pl.pallas_call(functools.partial(kernel, leaves, depth), out_shape=(field...  50.3 us
    unnamed x4, local copies, waits for them, and re-layouts  2.14 us

profile of v2, /device:TPU:0, one launch (start us, length us, event | category | flops | bytes accessed | tf_op | source)
XLA Modules:
  0.0 53.1 jit_solution(3366527684121581753)
XLA Ops:
  0.6 50.3 %shard_map.104 = (f32[2,32,256]{2,1,0:T(8,128)}, f32[2,32,256]{2,1,0:T(8,128)}) custom-call(s32[16]{0:T(128)} %bitcast.20, s32[16]{0:T(128)} %bitcast.21, f32[2,32,256]{2,1,0:T(8,128)} %bitcast.16, f32[2,32,256]{2,1,0:T(8,128)} %bitcast.17, f32[2,256,256]{2,1,0:T(8,128)} %bitcast.12, f32[2,16,32,256]{3,2,1,0:T(8,128)} %bitcast.11, f32[2,256,256]{2,1,0:T(8,128)} %bitcast.13, ...), custom_call_target="tpu_custom_call" | custom-call | tf_op jit(solution)/shard_map/pallas_call | solution.py:319
  51.0 0.0 copy-start
  51.0 1.5 %copy.13 = f32[1,1,2,32,256]{4,3,2,1,0:T(8,128)} copy(f32[1,1,2,32,256]{4,3,2,1,0:T(8,128)} %bitcast.19) | data formatting | bytes 131072
  52.5 0.0 copy-done
  52.5 0.6 %copy.14 = f32[1,1,2,32,256]{4,3,2,1,0:T(8,128)} copy(f32[1,1,2,32,256]{4,3,2,1,0:T(8,128)S(1)} %bitcast.18) | data formatting | bytes 131072
Async XLA Ops:
  51.0 1.5 %copy-start = (f32[2,32,256]{2,1,0:T(8,128)S(1)}, f32[2,32,256]{2,1,0:T(8,128)}, u32[]{:S(2)}) copy-start(f32[2,32,256]{2,1,0:T(8,128)} %get-tuple-element.5) | copy-start | bytes 196612

commit v3 on v2

--- a/solution.py
+++ b/solution.py
@@ -67,7 +67,7 @@
 def kernel(
     leaves, depth,
     tgt, off, s_down, s_up, leaf, coup, sep_far, top_far, bot_far,
-    out_down, out_up,
+    out,
     sep, j_top, j_bot,
     lw, cw, sw, jw, m1, m2, ybuf, ubuf, msend, marr, usend, uarr, rsend, rarr, tsend, tarr,
     ls, ms, mr, us, ur, rs, rr, ts, tr,
@@ -189,8 +189,8 @@
 
     def send_update(e, u):
         usend[e] = u.reshape(leaves, rb, width)
-        for out, _ in u_moves[e]:
-            out.start()
+        for going, _ in u_moves[e]:
+            going.start()
         uarr[e, me] = usend[e, me]
 
     def with_trace(e):
@@ -200,8 +200,8 @@
         ybuf[e] = ybuf[e] + apply_c(jw[0, d], jw[1, d], trace)
 
     pl.semaphore_wait(barrier, leaves - 1 + jnp.where(inward, 1, 0) + jnp.where(onward, 1, 0))
-    for out, _ in mask_moves:
-        out.start()
+    for going, _ in mask_moves:
+        going.start()
 
     @pl.when(jnp.logical_not(inner))
     def _():
@@ -245,8 +245,8 @@
             for b in range(1, qb):
                 reply = reply + x[b * rb:(b + 1) * rb] * marr[s, b:b + 1]
             rsend[e, s] = reply
-        for out, _ in r_moves[e]:
-            out.start()
+        for going, _ in r_moves[e]:
+            going.start()
         rarr[e, me] = rsend[e, me]
         if e == 0:
             chi, clo = twin(cw[0]), twin(cw[1])
@@ -280,19 +280,11 @@
             pass_on()
         else:
             pl.when(inner)(pass_on)
-        field = corrected(pl.ds(0, psize)).T[:lanes].reshape(2, cols, psize)
-
-        @pl.when(d == 0)
-        def _():
-            out_down[...] = field
-
-        @pl.when(d == 1)
-        def _():
-            out_up[...] = field
+        out[d] = corrected(pl.ds(0, psize)).T[:lanes].reshape(2, cols, psize)
 
     for moves in [mask_moves] + u_moves + r_moves:
-        for out, _ in moves:
-            out.wait_send()
+        for going, _ in moves:
+            going.wait_send()
     trace_move(0).wait_send()
 
     @pl.when(inner)
@@ -315,12 +307,11 @@
         vmem = pl.BlockSpec(memory_space=pltpu.VMEM)
         smem = pl.BlockSpec(memory_space=pltpu.SMEM)
         sems = pltpu.SemaphoreType.DMA
-        field = jax.ShapeDtypeStruct((2, cols, psize), F32)
-        down, up = pl.pallas_call(
+        fields = pl.pallas_call(
             functools.partial(kernel, leaves, depth),
-            out_shape=(field, field),
+            out_shape=jax.ShapeDtypeStruct((2, 2, cols, psize), F32),
             in_specs=[smem] * 2 + [vmem] * 4 + [pl.BlockSpec(memory_space=pl.ANY)] * 3,
-            out_specs=(vmem, vmem),
+            out_specs=vmem,
             scratch_shapes=[
                 pltpu.VMEM((2, qsize, qsize), F32),
                 pltpu.VMEM((2, tsize, psize), F32),
@@ -355,7 +346,7 @@
             s_down[0, 0], s_up[0, 0], leaf[0, 0], coup[0, 0].reshape(2, nb, rb, psize),
             sep[0, 0], j_top[0, 0], j_bot[0, 0],
         )
-        return down[None, None], up[None, None]
+        return fields[0][None, None], fields[1][None, None]
 
     five, four, three = (P("layer", "front", *([None] * k)) for k in (3, 2, 1))
     return jax.shard_map(

time: 53.3 us -> 52.5 us (0.985)
  local copies, waits for them, and re-layouts: 2.14 us -> 1.53 us
    unnamed x4 -> x0, local copies, waits for them, and re-layouts: 2.14 us -> none
    another operation x0 -> x1, local copies, waits for them, and re-layouts: none -> 1.53 us  [body(): return (fields[0][None, None], fields[1][None, None])]
where the time goes in v3:
time: 52.5 us; the launch traced here: 52.3 us
  Pallas kernels  50.1 us (95%)
  local copies, waits for them, and re-layouts  1.53 us (3%)
  between operations  0.64 us (1%)
    pallas_call x1, Pallas kernels, body(): pl.pallas_call(functools.partial(kernel, leaves, depth), out_shape=jax.Sh...  50.1 us
    another operation x1, local copies, waits for them, and re-layouts, body(): return (fields[0][None, None], fields[1][None, None])  1.53 us

profile of v3, /device:TPU:0, one launch (start us, length us, event | category | flops | bytes accessed | tf_op | source)
XLA Modules:
  0.0 52.3 jit_solution(15037512072620983253)
XLA Ops:
  0.6 50.1 %shard_map.104 = f32[2,2,32,256]{3,2,1,0:T(8,128)} custom-call(s32[16]{0:T(128)} %bitcast.20, s32[16]{0:T(128)} %bitcast.21, f32[2,32,256]{2,1,0:T(8,128)} %bitcast.18, f32[2,32,256]{2,1,0:T(8,128)} %bitcast.19, f32[2,256,256]{2,1,0:T(8,128)} %bitcast.14, f32[2,16,32,256]{3,2,1,0:T(8,128)} %bitcast.13, f32[2,256,256]{2,1,0:T(8,128)} %bitcast.15, ...), custom_call_target="tpu_custom_call" | custom-call | tf_op jit(solution)/shard_map/pallas_call | solution.py:310
  50.8 1.5 %slice_bitcast_fusion = (f32[1,1,2,32,256]{4,3,2,1,0:T(8,128)}, f32[1,1,2,32,256]{4,3,2,1,0:T(8,128)}) fusion(f32[2,2,32,256]{3,2,1,0:T(8,128)} %shard_map.104), kind=kLoop, calls=%fused_computation | loop fusion | bytes 262144 | tf_op jit(solution)/shard_map/broadcast_in_dim;squeeze | solution.py:349
